TPU v7x, 32 devices: a whole 2x2x4 slice. The times are simulated.
32 devices in a mesh: row: 4 (over y, x), col: 8 (over z, core).
Axes of the slice: x: 2, y: 2, z: 4, core: 2. Of those that a mesh axis runs over, the one named last changes fastest.
Arguments:
- trailing: float32 [3072, 3072], P('row', 'col'), may hold values from -6 to 6, as said below
- v_panels: bfloat16 [3, 3072, 256], P(None, ('row', 'col')), may hold values from -6 to 6
Outputs:
- updated: float32 [3072, 3072], P('row', 'col')
- w_panels: float32 [3, 3072, 256], P(None, ('row', 'col'))
Inputs may be any that keep to these rules, and one draw needn't show every extreme that they name: trailing is symmetric: entry (i, j) equals entry (j, i).
All inputs are finite; a program needn't handle non-finite values.
Results may differ from a plain program's by a relative error of at most 0.0003.
Values may be sent and summed in bfloat16 or wider, within the bound.
A program may use at most 64 MiB of HBM per device.

v0:
```python
import math
import jax
import jax.numpy as jnp
from jax import lax
from jax.sharding import PartitionSpec as P


def broadcast(value, axis, root):
    mine = lax.axis_index(axis) == root
    return lax.psum(jnp.where(mine, value, jnp.zeros_like(value)), axis)


def on_device(trailing, v_panels):
    rows_tile = trailing.shape[0]
    cols_tile = trailing.shape[1]
    count_row = lax.axis_size("row")
    full_order = rows_tile * count_row
    scaling = 1.0 / math.sqrt(full_order)
    group_ratio = rows_tile // cols_tile
    col_index = lax.axis_index("col")
    root_row = col_index // group_ratio
    offset = col_index % group_ratio * cols_tile
    ticks_all = v_panels.shape[0]
    highest = lax.Precision.HIGHEST
    v_rows_all = lax.all_gather(v_panels, "col", axis=1, tiled=True)
    v_mirror_all = broadcast(v_rows_all, "row", root_row)
    v_cols_all = lax.dynamic_slice_in_dim(v_mirror_all, offset, cols_tile, 1)
    current = trailing
    w_list = []
    for tick in range(ticks_all):
        v_rows = v_rows_all[tick]
        v_cols = v_cols_all[tick]
        v_rows_f = v_rows.astype(jnp.float32)
        v_cols_f = v_cols.astype(jnp.float32)
        block = current
        summed = lax.psum_scatter(
            jnp.dot(block, v_cols_f, precision=highest, preferred_element_type=jnp.float32),
            "col",
            scatter_dimension=0,
            tiled=True,
        )
        w_piece = summed * scaling
        w_rows = lax.all_gather(w_piece, "col", axis=0, tiled=True)
        w_mirror = broadcast(w_rows, "row", root_row)
        w_cols = lax.dynamic_slice_in_dim(w_mirror, offset, cols_tile, 0)
        rows_side = jnp.concatenate([v_rows_f, w_rows], axis=1)
        cols_side = jnp.concatenate([w_cols, v_cols_f], axis=1)
        update = lax.dot_general(
            rows_side,
            cols_side,
            (((1,), (1,)), ((), ())),
            precision=highest,
            preferred_element_type=jnp.float32,
        )
        current = current - update * (0.5 * scaling)
        w_list.append(w_piece)
    return (current, jnp.stack(w_list, axis=0))


def solution(mesh):
    in_specs = (P("row", "col"), P(None, ("row", "col"), None))
    out_specs = (P("row", "col"), P(None, ("row", "col"), None))
    return jax.shard_map(
        on_device, mesh=mesh, in_specs=in_specs, out_specs=out_specs, check_vma=False
    )
```

profile of v0, /device:TPU:0, one launch (start us, length us, event | category | flops | bytes accessed | tf_op | source)
XLA Modules:
  0.0 415.8 jit_solution(6455830931447291190)
XLA Ops:
  7.2 0.0 all-gather.2.cloned.1.call-start
  7.2 0.7 all-gather.2.cloned.1.call-update
  7.9 0.0 all-reduce.5.cloned.1.call-start
  8.0 27.2 %all-gather.2.cloned.1.call-done = bf16[3,768,256]{2,1,0:T(8,128)(2,1)} async-done(((bf16[3,96,256]{2,1,0:T(8,128)(2,1)}), bf16[3,768,256]{2,1,0:T(8,128)(2,1)}) %all-gather.2.cloned.1.call-update) | async-done | bytes 1179664 | tf_op jit(solution)/shard_map/all_gather | solution.py:25
  35.1 2.4 broadcast_select_fusion
  37.5 0.0 copy-start.1
  37.5 0.0 all-reduce.5.cloned.1.call-update
  37.5 0.0 reduce-scatter.10.cloned.1.call-start
  37.6 55.3 %all-reduce.5.cloned.1.call-done = bf16[3,768,256]{2,1,0:T(8,128)(2,1)} async-done(((bf16[3,768,256]{2,1,0:T(8,128)(2,1)}), bf16[3,768,256]{2,1,0:T(8,128)(2,1)}) %all-reduce.5.cloned.1.call-update) | async-done | bytes 1179664 | tf_op jit(solution)/shard_map/psum | solution.py:10
  92.8 0.0 copy-done.1
  92.8 1.8 convolution_bitcast_fusion
  94.7 1.1 copy.16
  95.8 0.0 reduce-scatter.10.cloned.1.call-update
  95.9 0.0 all-reduce.7.cloned.1.call-start
  95.9 31.9 %reduce-scatter.10.cloned.1.call-done = f32[96,256]{1,0:T(8,128)} async-done(((f32[768,256]{1,0:T(8,128)}), f32[96,256]{1,0:T(8,128)}) %reduce-scatter.10.cloned.1.call-update) | async-done | bytes 98320
  127.9 1.0 copy.17
  128.8 0.7 fusion.53
  129.5 0.1 copy.8
  129.6 15.7 %all_gather.13 = f32[768,256]{1,0:T(8,128)S(1)} all-gather(f32[96,256]{1,0:T(8,128)S(1)} %copy.8), channel_id=1, replica_groups=mesh['row'=4,'col'=8] {'col'}, dimensions={0}, use_global_device_ids=true | all-gather | bytes 884736 | tf_op jit(solution)/shard_map/all_gather | solution.py:43
  145.3 0.0 copy-start
  145.4 1.0 broadcast_select_fusion.3
  146.3 0.0 all-reduce.7.cloned.1.call-update
  146.3 0.0 reduce-scatter.12.cloned.1.call-start
  146.4 0.5 copy-done
  146.9 0.0 copy-start.4
  146.9 1.4 fusion.39
  148.4 0.5 copy-done.4
  148.9 1.0 fusion.45
  149.9 43.8 %all-reduce.7.cloned.1.call-done = f32[768,256]{1,0:T(8,128)} async-done(((f32[768,256]{1,0:T(8,128)}), f32[768,256]{1,0:T(8,128)}) %all-reduce.7.cloned.1.call-update) | async-done | bytes 786448 | tf_op jit(solution)/shard_map/psum | solution.py:10
  193.6 0.0 copy-start.3
  193.6 1.1 constant_dynamic-slice_fusion.2
  194.7 0.2 copy-done.3
  194.9 3.6 fusion.27
  198.5 2.6 fusion.44
  201.1 0.0 reduce-scatter.12.cloned.1.call-update
  201.1 0.0 all-reduce.9.cloned.1.call-start
  201.2 31.9 %reduce-scatter.12.cloned.1.call-done = f32[96,256]{1,0:T(8,128)} async-done(((f32[768,256]{1,0:T(8,128)}), f32[96,256]{1,0:T(8,128)}) %reduce-scatter.12.cloned.1.call-update) | async-done | bytes 98320
  233.1 1.0 copy.19
  234.1 0.7 fusion.54
  234.8 0.1 copy.10
  234.9 15.7 %all_gather.14 = f32[768,256]{1,0:T(8,128)S(1)} all-gather(f32[96,256]{1,0:T(8,128)S(1)} %copy.10), channel_id=1, replica_groups=mesh['row'=4,'col'=8] {'col'}, dimensions={0}, use_global_device_ids=true | all-gather | bytes 884736 | tf_op jit(solution)/shard_map/all_gather | solution.py:43
  250.6 0.9 broadcast_select_fusion.2
  251.5 0.0 all-reduce.9.cloned.1.call-update
  251.6 0.0 reduce-scatter.14.cloned.1.call-start
  251.6 47.2 %all-reduce.9.cloned.1.call-done = f32[768,256]{1,0:T(8,128)} async-done(((f32[768,256]{1,0:T(8,128)}), f32[768,256]{1,0:T(8,128)}) %all-reduce.9.cloned.1.call-update) | async-done | bytes 786448 | tf_op jit(solution)/shard_map/psum | solution.py:10
  298.8 1.0 constant_dynamic-slice_fusion.1
  299.8 3.9 fusion.21
  303.7 2.6 fusion.46
  306.3 0.0 reduce-scatter.14.cloned.1.call-update
  306.3 0.0 all-reduce.11.cloned.1.call-start
  306.4 31.9 %reduce-scatter.14.cloned.1.call-done = f32[96,256]{1,0:T(8,128)} async-done(((f32[768,256]{1,0:T(8,128)}), f32[96,256]{1,0:T(8,128)}) %reduce-scatter.14.cloned.1.call-update) | async-done | bytes 98320
  338.3 1.0 copy.21
  339.3 0.7 fusion.55
  340.0 0.1 copy.12
  340.1 15.9 %all_gather.15 = f32[768,256]{1,0:T(8,128)S(1)} all-gather(f32[96,256]{1,0:T(8,128)S(1)} %copy.12), channel_id=1, replica_groups=mesh['row'=4,'col'=8] {'col'}, dimensions={0}, use_global_device_ids=true | all-gather | bytes 884736 | tf_op jit(solution)/shard_map/all_gather | solution.py:43
  356.0 1.0 broadcast_select_fusion.1
  357.0 0.0 all-reduce.11.cloned.1.call-update
  357.0 0.0 copy-start.2
  357.0 1.1 pad_maximum_fusion
  358.1 0.9 copy.13
  359.0 45.2 %all-reduce.11.cloned.1.call-done = f32[768,256]{1,0:T(8,128)} async-done(((f32[768,256]{1,0:T(8,128)}), f32[768,256]{1,0:T(8,128)}) %all-reduce.11.cloned.1.call-update) | async-done | bytes 786448 | tf_op jit(solution)/shard_map/psum | solution.py:10
  404.3 1.0 constant_dynamic-slice_fusion
  405.3 0.0 copy-done.2
  405.3 3.6 fusion.15
Async XLA Ops:
  7.2 28.0 %all-gather.2.cloned.1.call-start = ((), (), s32[]{:S(2)}) async-start(), calls=%async_computation.3 | async-start | bytes 1327104 | tf_op jit(solution)/shard_map/all_gather | solution.py:25
  7.9 84.9 %all-reduce.5.cloned.1.call-start = ((), (), s32[]{:S(2)}) async-start(), calls=%async_computation.4 | async-start | bytes 2359296 | tf_op jit(solution)/shard_map/psum | solution.py:10
  37.5 55.4 %copy-start.1 = (f32[768,384]{1,0:T(8,128)S(1)}, f32[768,384]{1,0:T(8,128)}, u32[]{:S(2)}) copy-start(f32[768,384]{1,0:T(8,128)} %param.2) | copy-start | bytes 3538948
  37.5 90.3 %reduce-scatter.10.cloned.1.call-start = ((), (), s32[]{:S(2)}) async-start(), calls=%async_computation.8 | async-start | bytes 884736
  95.9 97.8 %all-reduce.7.cloned.1.call-start = ((), (), s32[]{:S(2)}) async-start(), calls=%async_computation.5 | async-start | bytes 1572864 | tf_op jit(solution)/shard_map/psum | solution.py:10
  145.3 1.6 copy-start
  146.3 86.8 %reduce-scatter.12.cloned.1.call-start = ((), (), s32[]{:S(2)}) async-start(), calls=%async_computation.9 | async-start | bytes 884736
  146.9 2.0 copy-start.4
  193.6 1.3 copy-start.3
  201.1 97.7 %all-reduce.9.cloned.1.call-start = ((), (), s32[]{:S(2)}) async-start(), calls=%async_computation.6 | async-start | bytes 1572864 | tf_op jit(solution)/shard_map/psum | solution.py:10
  251.6 86.8 %reduce-scatter.14.cloned.1.call-start = ((), (), s32[]{:S(2)}) async-start(), calls=%async_computation.10 | async-start | bytes 884736
  306.3 97.9 %all-reduce.11.cloned.1.call-start = ((), (), s32[]{:S(2)}) async-start(), calls=%async_computation.7 | async-start | bytes 1572864 | tf_op jit(solution)/shard_map/psum | solution.py:10
  357.0 48.3 %copy-start.2 = (f32[768,256]{1,0:T(8,128)S(1)}, f32[768,256]{1,0:T(8,128)}, u32[]{:S(2)}) copy-start(f32[768,256]{1,0:T(8,128)} %get-tuple-element.9) | copy-start | bytes 2359300
Sparse Core Ops, SparseCore 0:
  9.6 25.4 all-gather.1
  38.8 53.9 all-reduce.4
  96.0 31.8 reduce-scatter.9
  146.5 47.1 all-reduce.6
  201.2 31.8 reduce-scatter.11
  251.7 47.1 all-reduce.8
  306.5 31.8 reduce-scatter.13
  357.1 47.1 all-reduce.10
where the time goes:
time: 416 us
  waiting for transfers between devices  315 us (76%)
  blocking collectives  47.4 us (11%)
  matrix products  18.1 us (4%)
  between operations  14.3 us (3%)
  other arithmetic  10.8 us (3%)
  local copies, waits for them, and re-layouts  9.55 us (2%)
    psum x4, waiting for transfers between devices, broadcast(): return lax.psum(jnp.where(mine, value, jnp.zeros_like(value)), axis)  192 us
    unnamed x11, waiting for transfers between devices  96.6 us
    all_gather x3, blocking collectives, on_device(): w_rows = lax.all_gather(w_piece, 'col', axis=0, tiled=True)  47.4 us
    all_gather x1, waiting for transfers between devices, on_device(): v_rows_all = lax.all_gather(v_panels, 'col', axis=1, tiled=True)  27.2 us
    dot_general x3, matrix products, on_device(): lax.dot_general(rows_side, cols_side, (((1,), (1,)), ((), ())), precision...  11.1 us
  transfers between devices with their start and end apart: 8, of which 8 were waited for; matrix products, arithmetic and copies ran while one was open for 1% of the time, Pallas kernels for 0%

commit v1 on v0

--- a/solution.py
+++ b/solution.py
@@ -40,7 +40,26 @@
             tiled=True,
         )
         w_piece = summed * scaling
-        w_rows = lax.all_gather(w_piece, "col", axis=0, tiled=True)
+        peers, mine_2, rows = (lax.axis_size("col"), lax.axis_index("col"), w_piece.shape[0])
+        forward = [(i, (i + 1) % peers) for i in range(peers)]
+        behind = [(i, (i - 1) % peers) for i in range(peers)]
+        whole = jnp.zeros(
+            (*w_piece.shape[:0], peers * rows, *w_piece.shape[0 + 1 :]), w_piece.dtype
+        )
+        whole = lax.dynamic_update_slice_in_dim(whole, w_piece, mine_2 * rows, axis=0)
+        from_left = from_right = w_piece
+        half = peers // 2
+        for turn in range(1, half + 1):
+            from_left = lax.ppermute(from_left, "col", forward)
+            whole = lax.dynamic_update_slice_in_dim(
+                whole, from_left, (mine_2 - turn) % peers * rows, axis=0
+            )
+            if turn < peers - half:
+                from_right = lax.ppermute(from_right, "col", behind)
+                whole = lax.dynamic_update_slice_in_dim(
+                    whole, from_right, (mine_2 + turn) % peers * rows, axis=0
+                )
+        w_rows = whole
         w_mirror = broadcast(w_rows, "row", root_row)
         w_cols = lax.dynamic_slice_in_dim(w_mirror, offset, cols_tile, 0)
         rows_side = jnp.concatenate([v_rows_f, w_rows], axis=1)

time: 416 us -> 446 us (1.072)
  blocking collectives: 47.4 us -> 0 us
  waiting for transfers between devices: 315 us -> 356 us
  starting transfers between devices: 0.33 us -> 33.2 us
    all_gather x3 -> x0, blocking collectives: 47.4 us -> none  [on_device(): w_rows = lax.all_gather(w_piece, 'col', axis=0, tiled=True)]
    ppermute x0 -> x21, waiting for transfers between devices: none -> 41.6 us  [the longest x12 41.6 us: on_device(): from_left = lax.ppermute(from_left, 'col', forward)]
    ppermute x0 -> x21, starting transfers between devices: none -> 32.7 us  [the longest x9 32 us: on_device(): from_right = lax.ppermute(from_right, 'col', behind)]
  transfers between devices with their start and end apart: 8 -> 29, of which waited for: 8 -> 20; matrix products, arithmetic and copies ran while one was open for 1% -> 1% of each run, Pallas kernels for 0% -> 0%
where the time goes in v1:
time: 446 us; the launch traced here: 445 us
  waiting for transfers between devices  356 us (80%)
  starting transfers between devices  33.2 us (7%)
  matrix products  18.1 us (4%)
  between operations  14.9 us (3%)
  local copies, waits for them, and re-layouts  11.8 us (3%)
  other arithmetic  10.9 us (2%)
    psum x4, waiting for transfers between devices, broadcast(): return lax.psum(jnp.where(mine, value, jnp.zeros_like(value)), axis)  191 us
    unnamed x11, waiting for transfers between devices  96.5 us
    ppermute x12, waiting for transfers between devices, on_device(): from_left = lax.ppermute(from_left, 'col', forward)  41.6 us
    ppermute x9, starting transfers between devices, on_device(): from_right = lax.ppermute(from_right, 'col', behind)  32 us
    all_gather x1, waiting for transfers between devices, on_device(): v_rows_all = lax.all_gather(v_panels, 'col', axis=1, tiled=True)  27.2 us
    dot_general x3, matrix products, on_device(): lax.dot_general(rows_side, cols_side, (((1,), (1,)), ((), ())), precision...  11.1 us
  transfers between devices with their start and end apart: 29, of which 20 were waited for; matrix products, arithmetic and copies ran while one was open for 1% of the time, Pallas kernels for 0%

profile of v1, /device:TPU:0, one launch (start us, length us, event | category | flops | bytes accessed | tf_op | source)
XLA Modules:
  0.0 445.2 jit_solution(2246876678098563205)
XLA Ops:
  7.2 0.7 all-gather.2.cloned.1.call-update
  8.0 27.2 %all-gather.2.cloned.1.call-done = bf16[3,768,256]{2,1,0:T(8,128)(2,1)} async-done(((bf16[3,96,256]{2,1,0:T(8,128)(2,1)}), bf16[3,768,256]{2,1,0:T(8,128)(2,1)}) %all-gather.2.cloned.1.call-update) | async-done | bytes 1179664 | tf_op jit(solution)/shard_map/all_gather | solution.py:25
  35.1 2.4 broadcast_select_fusion
  37.6 55.3 %all-reduce.5.cloned.1.call-done = bf16[3,768,256]{2,1,0:T(8,128)(2,1)} async-done(((bf16[3,768,256]{2,1,0:T(8,128)(2,1)}), bf16[3,768,256]{2,1,0:T(8,128)(2,1)}) %all-reduce.5.cloned.1.call-update) | async-done | bytes 1179664 | tf_op jit(solution)/shard_map/psum | solution.py:10
  92.8 1.8 convolution_bitcast_fusion
  94.7 1.1 copy.60
  96.0 31.8 %reduce-scatter.10.cloned.1.call-done = f32[96,256]{1,0:T(8,128)} async-done(((f32[768,256]{1,0:T(8,128)}), f32[96,256]{1,0:T(8,128)}) %reduce-scatter.10.cloned.1.call-update) | async-done | bytes 98320
  127.9 1.0 copy.61
  128.8 0.7 fusion.53
  129.7 3.5 collective-permute-start.1
  133.3 2.7 collective-permute-done
  136.3 3.6 collective-permute-start.3
  139.9 2.7 collective-permute-done.2
  142.7 0.1 copy.35
  142.8 3.6 collective-permute-start.5
  146.4 2.5 collective-permute-done.4
  149.1 0.1 copy.37
  149.2 6.0 %collective-permute-done.6 = f32[96,256]{0,1:T(8,128)S(1)} collective-permute-done((f32[96,256]{0,1:T(8,128)S(1)}, f32[96,256]{0,1:T(8,128)S(1)}, u32[]{:S(2)}, u32[]{:S(2)}) %collective-permute-start.6) | collective-permute-done | bytes 98336 | tf_op jit(solution)/shard_map/ppermute | solution.py:53
  155.3 0.9 broadcast_select_fusion.3
  156.3 0.5 copy-done
  156.9 1.5 fusion.39
  158.4 0.5 copy-done.4
  158.8 1.0 fusion.45
  159.8 43.7 %all-reduce.7.cloned.1.call-done = f32[768,256]{1,0:T(8,128)} async-done(((f32[768,256]{1,0:T(8,128)}), f32[768,256]{1,0:T(8,128)}) %all-reduce.7.cloned.1.call-update) | async-done | bytes 786448 | tf_op jit(solution)/shard_map/psum | solution.py:10
  203.5 1.1 constant_dynamic-slice_fusion.2
  204.6 0.2 copy-done.3
  204.7 3.6 fusion.27
  208.4 2.6 fusion.44
  211.0 31.9 %reduce-scatter.12.cloned.1.call-done = f32[96,256]{1,0:T(8,128)} async-done(((f32[768,256]{1,0:T(8,128)}), f32[96,256]{1,0:T(8,128)}) %reduce-scatter.12.cloned.1.call-update) | async-done | bytes 98320
  243.0 1.0 copy.63
  243.9 0.7 fusion.54
  244.8 3.5 collective-permute-start.8
  248.4 2.7 collective-permute-done.7
  251.4 3.6 collective-permute-start.10
  255.0 2.7 collective-permute-done.9
  257.8 0.1 copy.44
  257.9 3.6 collective-permute-start.12
  261.5 2.5 collective-permute-done.11
  264.2 0.1 copy.46
  264.3 6.0 %collective-permute-done.13 = f32[96,256]{0,1:T(8,128)S(1)} collective-permute-done((f32[96,256]{0,1:T(8,128)S(1)}, f32[96,256]{0,1:T(8,128)S(1)}, u32[]{:S(2)}, u32[]{:S(2)}) %collective-permute-start.13) | collective-permute-done | bytes 98336 | tf_op jit(solution)/shard_map/ppermute | solution.py:53
  270.4 0.9 broadcast_select_fusion.2
  271.4 0.2 reduce-scatter.14.cloned.1.call-start
  271.6 46.9 %all-reduce.9.cloned.1.call-done = f32[768,256]{1,0:T(8,128)} async-done(((f32[768,256]{1,0:T(8,128)}), f32[768,256]{1,0:T(8,128)}) %all-reduce.9.cloned.1.call-update) | async-done | bytes 786448 | tf_op jit(solution)/shard_map/psum | solution.py:10
  318.6 1.0 constant_dynamic-slice_fusion.1
  319.6 3.9 fusion.21
  323.4 2.6 fusion.46
  326.1 31.9 %reduce-scatter.14.cloned.1.call-done = f32[96,256]{1,0:T(8,128)} async-done(((f32[768,256]{1,0:T(8,128)}), f32[96,256]{1,0:T(8,128)}) %reduce-scatter.14.cloned.1.call-update) | async-done | bytes 98320
  358.0 1.0 copy.65
  359.0 0.7 fusion.55
  359.9 3.5 collective-permute-start.15
  363.5 2.7 collective-permute-done.14
  366.4 0.1 copy.51
  366.5 3.6 collective-permute-start.17
  370.1 2.7 collective-permute-done.16
  372.9 0.1 copy.53
  373.0 3.6 collective-permute-start.19
  376.6 2.5 collective-permute-done.18
  379.4 6.0 %collective-permute-done.20 = f32[96,256]{0,1:T(8,128)S(1)} collective-permute-done((f32[96,256]{0,1:T(8,128)S(1)}, f32[96,256]{0,1:T(8,128)S(1)}, u32[]{:S(2)}, u32[]{:S(2)}) %collective-permute-start.20) | collective-permute-done | bytes 98336 | tf_op jit(solution)/shard_map/ppermute | solution.py:53
  385.5 1.0 broadcast_select_fusion.1
  386.5 1.1 pad_maximum_fusion
  387.7 0.9 copy.57
  388.5 45.1 %all-reduce.11.cloned.1.call-done = f32[768,256]{1,0:T(8,128)} async-done(((f32[768,256]{1,0:T(8,128)}), f32[768,256]{1,0:T(8,128)}) %all-reduce.11.cloned.1.call-update) | async-done | bytes 786448 | tf_op jit(solution)/shard_map/psum | solution.py:10
  433.7 1.0 constant_dynamic-slice_fusion
  434.7 3.6 fusion.15
  (87 shorter events, 3.1 us)
Async XLA Ops:
  7.2 28.0 %all-gather.2.cloned.1.call-start = ((), (), s32[]{:S(2)}) async-start(), calls=%async_computation.3 | async-start | bytes 1327104 | tf_op jit(solution)/shard_map/all_gather | solution.py:25
  7.9 84.9 %all-reduce.5.cloned.1.call-start = ((), (), s32[]{:S(2)}) async-start(), calls=%async_computation.4 | async-start | bytes 2359296 | tf_op jit(solution)/shard_map/psum | solution.py:10
  37.5 55.4 %copy-start.1 = (f32[768,384]{1,0:T(8,128)S(1)}, f32[768,384]{1,0:T(8,128)}, u32[]{:S(2)}) copy-start(f32[768,384]{1,0:T(8,128)} %param.2) | copy-start | bytes 3538948
  37.5 90.3 %reduce-scatter.10.cloned.1.call-start = ((), (), s32[]{:S(2)}) async-start(), calls=%async_computation.8 | async-start | bytes 884736
  95.9 107.6 %all-reduce.7.cloned.1.call-start = ((), (), s32[]{:S(2)}) async-start(), calls=%async_computation.5 | async-start | bytes 1572864 | tf_op jit(solution)/shard_map/psum | solution.py:10
  129.6 6.4 %collective-permute-start = (f32[96,256]{0,1:T(8,128)S(1)}, f32[96,256]{0,1:T(8,128)S(1)}, u32[]{:S(2)}, u32[]{:S(2)}) collective-permute-start(f32[96,256]{0,1:T(8,128)S(1)} %get-tuple-element.13), channel_id=1, source_target_pairs={{0,1},{1,2},{2,3},{3,4},{4,5},{5,6},{6,7},{7,0},{8,9},{9,10},{10,1... | collective-permute-start | bytes 294920 | tf_op jit(solution)/shard_map/ppermute | solution.py:53
  129.7 6.5 %collective-permute-start.1 = (f32[96,256]{0,1:T(8,128)S(1)}, f32[96,256]{0,1:T(8,128)S(1)}, u32[]{:S(2)}, u32[]{:S(2)}) collective-permute-start(f32[96,256]{0,1:T(8,128)S(1)} %get-tuple-element.13), channel_id=1, source_target_pairs={{0,7},{1,0},{2,1},{3,2},{4,3},{5,4},{6,5},{7,6},{8,15},{9,8},{10,9... | collective-permute-start | bytes 294920 | tf_op jit(solution)/shard_map/ppermute | solution.py:58
  136.1 6.4 %collective-permute-start.2 = (f32[96,256]{0,1:T(8,128)S(1)}, f32[96,256]{0,1:T(8,128)S(1)}, u32[]{:S(2)}, u32[]{:S(2)}) collective-permute-start(f32[96,256]{0,1:T(8,128)S(1)} %collective-permute-done), channel_id=1, source_target_pairs={{0,1},{1,2},{2,3},{3,4},{4,5},{5,6},{6,7},{7,0},{8,9},{9,10},{10,1... | collective-permute-start | bytes 294920 | tf_op jit(solution)/shard_map/ppermute | solution.py:53
  136.3 6.4 %collective-permute-start.3 = (f32[96,256]{0,1:T(8,128)S(1)}, f32[96,256]{0,1:T(8,128)S(1)}, u32[]{:S(2)}, u32[]{:S(2)}) collective-permute-start(f32[96,256]{0,1:T(8,128)S(1)} %collective-permute-done.1), channel_id=1, source_target_pairs={{0,7},{1,0},{2,1},{3,2},{4,3},{5,4},{6,5},{7,6},{8,15},{9,8},{10,9... | collective-permute-start | bytes 294920 | tf_op jit(solution)/shard_map/ppermute | solution.py:58
  142.6 6.2 %collective-permute-start.4 = (f32[96,256]{0,1:T(8,128)S(1)}, f32[96,256]{0,1:T(8,128)S(1)}, u32[]{:S(2)}, u32[]{:S(2)}) collective-permute-start(f32[96,256]{0,1:T(8,128)S(1)} %collective-permute-done.2), channel_id=1, source_target_pairs={{0,1},{1,2},{2,3},{3,4},{4,5},{5,6},{6,7},{7,0},{8,9},{9,10},{10,1... | collective-permute-start | bytes 294920 | tf_op jit(solution)/shard_map/ppermute | solution.py:53
  142.8 6.2 %collective-permute-start.5 = (f32[96,256]{0,1:T(8,128)S(1)}, f32[96,256]{0,1:T(8,128)S(1)}, u32[]{:S(2)}, u32[]{:S(2)}) collective-permute-start(f32[96,256]{0,1:T(8,128)S(1)} %collective-permute-done.3), channel_id=1, source_target_pairs={{0,7},{1,0},{2,1},{3,2},{4,3},{5,4},{6,5},{7,6},{8,15},{9,8},{10,9... | collective-permute-start | bytes 294920 | tf_op jit(solution)/shard_map/ppermute | solution.py:58
  149.0 6.2 %collective-permute-start.6 = (f32[96,256]{0,1:T(8,128)S(1)}, f32[96,256]{0,1:T(8,128)S(1)}, u32[]{:S(2)}, u32[]{:S(2)}) collective-permute-start(f32[96,256]{0,1:T(8,128)S(1)} %collective-permute-done.4), channel_id=1, source_target_pairs={{0,1},{1,2},{2,3},{3,4},{4,5},{5,6},{6,7},{7,0},{8,9},{9,10},{10,1... | collective-permute-start | bytes 294920 | tf_op jit(solution)/shard_map/ppermute | solution.py:53
  155.3 1.6 copy-start
  156.3 86.7 %reduce-scatter.12.cloned.1.call-start = ((), (), s32[]{:S(2)}) async-start(), calls=%async_computation.9 | async-start | bytes 884736
  156.9 2.0 copy-start.4
  203.5 1.3 copy-start.3
  211.0 107.6 %all-reduce.9.cloned.1.call-start = ((), (), s32[]{:S(2)}) async-start(), calls=%async_computation.6 | async-start | bytes 1572864 | tf_op jit(solution)/shard_map/psum | solution.py:10
  244.7 6.4 %collective-permute-start.7 = (f32[96,256]{0,1:T(8,128)S(1)}, f32[96,256]{0,1:T(8,128)S(1)}, u32[]{:S(2)}, u32[]{:S(2)}) collective-permute-start(f32[96,256]{0,1:T(8,128)S(1)} %get-tuple-element.15), channel_id=1, source_target_pairs={{0,1},{1,2},{2,3},{3,4},{4,5},{5,6},{6,7},{7,0},{8,9},{9,10},{10,1... | collective-permute-start | bytes 294920 | tf_op jit(solution)/shard_map/ppermute | solution.py:53
  244.8 6.5 %collective-permute-start.8 = (f32[96,256]{0,1:T(8,128)S(1)}, f32[96,256]{0,1:T(8,128)S(1)}, u32[]{:S(2)}, u32[]{:S(2)}) collective-permute-start(f32[96,256]{0,1:T(8,128)S(1)} %get-tuple-element.15), channel_id=1, source_target_pairs={{0,7},{1,0},{2,1},{3,2},{4,3},{5,4},{6,5},{7,6},{8,15},{9,8},{10,9... | collective-permute-start | bytes 294920 | tf_op jit(solution)/shard_map/ppermute | solution.py:58
  251.2 6.4 %collective-permute-start.9 = (f32[96,256]{0,1:T(8,128)S(1)}, f32[96,256]{0,1:T(8,128)S(1)}, u32[]{:S(2)}, u32[]{:S(2)}) collective-permute-start(f32[96,256]{0,1:T(8,128)S(1)} %collective-permute-done.7), channel_id=1, source_target_pairs={{0,1},{1,2},{2,3},{3,4},{4,5},{5,6},{6,7},{7,0},{8,9},{9,10},{10,1... | collective-permute-start | bytes 294920 | tf_op jit(solution)/shard_map/ppermute | solution.py:53
  251.4 6.4 %collective-permute-start.10 = (f32[96,256]{0,1:T(8,128)S(1)}, f32[96,256]{0,1:T(8,128)S(1)}, u32[]{:S(2)}, u32[]{:S(2)}) collective-permute-start(f32[96,256]{0,1:T(8,128)S(1)} %collective-permute-done.8), channel_id=1, source_target_pairs={{0,7},{1,0},{2,1},{3,2},{4,3},{5,4},{6,5},{7,6},{8,15},{9,8},{10,9... | collective-permute-start | bytes 294920 | tf_op jit(solution)/shard_map/ppermute | solution.py:58
  257.7 6.2 %collective-permute-start.11 = (f32[96,256]{0,1:T(8,128)S(1)}, f32[96,256]{0,1:T(8,128)S(1)}, u32[]{:S(2)}, u32[]{:S(2)}) collective-permute-start(f32[96,256]{0,1:T(8,128)S(1)} %collective-permute-done.9), channel_id=1, source_target_pairs={{0,1},{1,2},{2,3},{3,4},{4,5},{5,6},{6,7},{7,0},{8,9},{9,10},{10,1... | collective-permute-start | bytes 294920 | tf_op jit(solution)/shard_map/ppermute | solution.py:53
  257.9 6.2 %collective-permute-start.12 = (f32[96,256]{0,1:T(8,128)S(1)}, f32[96,256]{0,1:T(8,128)S(1)}, u32[]{:S(2)}, u32[]{:S(2)}) collective-permute-start(f32[96,256]{0,1:T(8,128)S(1)} %collective-permute-done.10), channel_id=1, source_target_pairs={{0,7},{1,0},{2,1},{3,2},{4,3},{5,4},{6,5},{7,6},{8,15},{9,8},{10,9... | collective-permute-start | bytes 294920 | tf_op jit(solution)/shard_map/ppermute | solution.py:58
  264.1 6.2 %collective-permute-start.13 = (f32[96,256]{0,1:T(8,128)S(1)}, f32[96,256]{0,1:T(8,128)S(1)}, u32[]{:S(2)}, u32[]{:S(2)}) collective-permute-start(f32[96,256]{0,1:T(8,128)S(1)} %collective-permute-done.11), channel_id=1, source_target_pairs={{0,1},{1,2},{2,3},{3,4},{4,5},{5,6},{6,7},{7,0},{8,9},{9,10},{10,1... | collective-permute-start | bytes 294920 | tf_op jit(solution)/shard_map/ppermute | solution.py:53
  271.4 86.6 %reduce-scatter.14.cloned.1.call-start = ((), (), s32[]{:S(2)}) async-start(), calls=%async_computation.10 | async-start | bytes 884736
  326.0 107.6 %all-reduce.11.cloned.1.call-start = ((), (), s32[]{:S(2)}) async-start(), calls=%async_computation.7 | async-start | bytes 1572864 | tf_op jit(solution)/shard_map/psum | solution.py:10
  359.8 6.4 %collective-permute-start.14 = (f32[96,256]{0,1:T(8,128)S(1)}, f32[96,256]{0,1:T(8,128)S(1)}, u32[]{:S(2)}, u32[]{:S(2)}) collective-permute-start(f32[96,256]{0,1:T(8,128)S(1)} %get-tuple-element.17), channel_id=1, source_target_pairs={{0,1},{1,2},{2,3},{3,4},{4,5},{5,6},{6,7},{7,0},{8,9},{9,10},{10,1... | collective-permute-start | bytes 294920 | tf_op jit(solution)/shard_map/ppermute | solution.py:53
  359.9 6.5 %collective-permute-start.15 = (f32[96,256]{0,1:T(8,128)S(1)}, f32[96,256]{0,1:T(8,128)S(1)}, u32[]{:S(2)}, u32[]{:S(2)}) collective-permute-start(f32[96,256]{0,1:T(8,128)S(1)} %get-tuple-element.17), channel_id=1, source_target_pairs={{0,7},{1,0},{2,1},{3,2},{4,3},{5,4},{6,5},{7,6},{8,15},{9,8},{10,9... | collective-permute-start | bytes 294920 | tf_op jit(solution)/shard_map/ppermute | solution.py:58
  366.3 6.4 %collective-permute-start.16 = (f32[96,256]{0,1:T(8,128)S(1)}, f32[96,256]{0,1:T(8,128)S(1)}, u32[]{:S(2)}, u32[]{:S(2)}) collective-permute-start(f32[96,256]{0,1:T(8,128)S(1)} %collective-permute-done.14), channel_id=1, source_target_pairs={{0,1},{1,2},{2,3},{3,4},{4,5},{5,6},{6,7},{7,0},{8,9},{9,10},{10,1... | collective-permute-start | bytes 294920 | tf_op jit(solution)/shard_map/ppermute | solution.py:53
  366.5 6.4 %collective-permute-start.17 = (f32[96,256]{0,1:T(8,128)S(1)}, f32[96,256]{0,1:T(8,128)S(1)}, u32[]{:S(2)}, u32[]{:S(2)}) collective-permute-start(f32[96,256]{0,1:T(8,128)S(1)} %collective-permute-done.15), channel_id=1, source_target_pairs={{0,7},{1,0},{2,1},{3,2},{4,3},{5,4},{6,5},{7,6},{8,15},{9,8},{10,9... | collective-permute-start | bytes 294920 | tf_op jit(solution)/shard_map/ppermute | solution.py:58
  372.8 6.2 %collective-permute-start.18 = (f32[96,256]{0,1:T(8,128)S(1)}, f32[96,256]{0,1:T(8,128)S(1)}, u32[]{:S(2)}, u32[]{:S(2)}) collective-permute-start(f32[96,256]{0,1:T(8,128)S(1)} %collective-permute-done.16), channel_id=1, source_target_pairs={{0,1},{1,2},{2,3},{3,4},{4,5},{5,6},{6,7},{7,0},{8,9},{9,10},{10,1... | collective-permute-start | bytes 294920 | tf_op jit(solution)/shard_map/ppermute | solution.py:53
  373.0 6.2 %collective-permute-start.19 = (f32[96,256]{0,1:T(8,128)S(1)}, f32[96,256]{0,1:T(8,128)S(1)}, u32[]{:S(2)}, u32[]{:S(2)}) collective-permute-start(f32[96,256]{0,1:T(8,128)S(1)} %collective-permute-done.17), channel_id=1, source_target_pairs={{0,7},{1,0},{2,1},{3,2},{4,3},{5,4},{6,5},{7,6},{8,15},{9,8},{10,9... | collective-permute-start | bytes 294920 | tf_op jit(solution)/shard_map/ppermute | solution.py:58
  379.2 6.2 %collective-permute-start.20 = (f32[96,256]{0,1:T(8,128)S(1)}, f32[96,256]{0,1:T(8,128)S(1)}, u32[]{:S(2)}, u32[]{:S(2)}) collective-permute-start(f32[96,256]{0,1:T(8,128)S(1)} %collective-permute-done.18), channel_id=1, source_target_pairs={{0,1},{1,2},{2,3},{3,4},{4,5},{5,6},{6,7},{7,0},{8,9},{9,10},{10,1... | collective-permute-start | bytes 294920 | tf_op jit(solution)/shard_map/ppermute | solution.py:53
  386.5 48.2 %copy-start.2 = (f32[768,256]{1,0:T(8,128)S(1)}, f32[768,256]{1,0:T(8,128)}, u32[]{:S(2)}) copy-start(f32[768,256]{1,0:T(8,128)} %get-tuple-element.9) | copy-start | bytes 2359300
Sparse Core Ops, SparseCore 0:
  9.6 25.4 all-gather.1
  38.8 53.9 all-reduce.4
  96.0 31.8 reduce-scatter.9
  156.4 47.0 all-reduce.6
  211.1 31.8 reduce-scatter.11
  271.5 46.9 all-reduce.8
  326.1 31.8 reduce-scatter.13
  386.6 46.9 all-reduce.10
